TPU v7x, 256 devices: a whole 4x4x8 slice. The times are simulated.
256 devices in a mesh: chain: 64 (over z, y, core), col: 4 (over x).
Axes of the slice: x: 4, y: 4, z: 8, core: 2. Of those that a mesh axis runs over, the one named last changes fastest.
Arguments:
- diagonal_blocks: float32 [192, 256, 256], P('chain', 'col'), may hold values from -2 to 6, as said below
- couplings: float32 [192, 256, 256], P('chain', 'col'), may hold values from -2 to 2
- right_sides: float32 [64, 192, 256], P('col', 'chain'), may hold values from -0.04 to 0.04
Outputs:
- solution: float32 [64, 192, 256], P('col', 'chain')
Inputs may be any that keep to these rules, and one draw needn't show every extreme that they name: `diagonal_blocks`: each block is symmetric, and the block-tridiagonal matrix that the diagonal blocks form with the couplings is positive definite with every eigenvalue 0.0003 or more.
All inputs are finite; a program needn't handle non-finite values.
Results may differ from a plain program's by a relative error of at most 0.0003.
Values sent between devices are 32-bit elements; how exact they have to be, the bound alone decides.
A program may use at most 64 MiB of HBM per device.

v0:
```python
import jax
import jax.numpy as jnp
from jax import lax
from jax.sharding import PartitionSpec as P

finest = lax.Precision.HIGHEST


def passed_along(shard, axis, by):
    size = lax.axis_size(axis)
    pairs = [(i, i + by) for i in range(size) if 0 <= i + by < size]
    return lax.ppermute(shard, axis, pairs)


def matmul(first_factor, second_factor):
    return jnp.dot(first_factor, second_factor, precision=finest)


def invert(matrix):
    lower_factor = jnp.linalg.cholesky(matrix)
    identity = jnp.eye(matrix.shape[0], dtype=matrix.dtype)
    return jax.scipy.linalg.cho_solve((lower_factor, True), identity)


def interior_solve(loads, inverses, products, inner_coups):
    before = jnp.concatenate([jnp.zeros_like(inner_coups), inner_coups], axis=0)

    def interior_forward(solved_prev, entries):
        load_now, coup_prev, inverse_now = entries
        reduced = load_now - matmul(solved_prev, coup_prev)
        solved_now = matmul(reduced, inverse_now.T)
        return (solved_now, solved_now)

    _, solved = lax.scan(interior_forward, jnp.zeros_like(loads[0]), (loads, before, inverses))

    def interior_backward(after, entries):
        solved_now, product = entries
        current = solved_now - matmul(after, product.T)
        return (current, current)

    _, earlier = lax.scan(interior_backward, solved[-1], (solved[:-1], products), reverse=True)
    return jnp.concatenate([earlier, solved[-1:]], axis=0)


def per_device(diagonal_blocks, couplings, right_sides):
    slab_count = diagonal_blocks.shape[0]
    col_width = diagonal_blocks.shape[1]
    inner_count = slab_count - 1
    col_start = lax.axis_index("col") * col_width
    chain_count = lax.axis_size("chain")
    levels = chain_count.bit_length() - 1
    full_diag, full_coup = (
        lax.all_gather(diagonal_blocks[:inner_count], "col", axis=1, tiled=True),
        lax.all_gather(couplings, "col", axis=1, tiled=True),
    )

    def body_forward(inverse_prev, entries):
        diag_now, coup_prev = entries
        product = matmul(inverse_prev, coup_prev)
        inverse_now = invert(diag_now - matmul(coup_prev.T, product))
        return (inverse_now, (inverse_prev, product))

    last_inverse, (early_inverses, products) = lax.scan(
        body_forward, invert(full_diag[0]), (full_diag[1:], full_coup[: inner_count - 1])
    )
    inverses = jnp.concatenate([early_inverses, last_inverse[None]], axis=0)
    inner_coups = full_coup[: inner_count - 1]
    coup_last = full_coup[inner_count - 1]
    coup_sep = full_coup[inner_count]
    last_cols = lax.dynamic_slice_in_dim(coup_last, col_start, col_width, 1)
    tail_start = matmul(last_inverse, last_cols)

    def body_backward(state, entries):
        green_block, tail_block = state
        inverse_now, product = entries
        green_block = inverse_now + matmul(matmul(product, green_block), product.T)
        tail_block = -matmul(product, tail_block)
        return ((green_block, tail_block), None)

    (near_green, near_tail), _ = lax.scan(
        body_backward, (last_inverse, tail_start), (early_inverses, products), reverse=True
    )
    loads = jnp.swapaxes(right_sides, 0, 1)
    interior = interior_solve(loads[:inner_count], inverses, products, inner_coups)
    got_green, got_tail, got_first = passed_along((near_green, near_tail, interior[0]), "chain", -1)
    sep_rows = lax.dynamic_slice_in_dim(coup_sep, col_start, col_width, 0)
    own_block = diagonal_blocks[inner_count].T
    b_part = (
        own_block
        - matmul(coup_last.T, tail_start)
        - matmul(coup_sep, matmul(got_green, sep_rows.T))
    )
    c_part = -matmul(coup_sep, got_tail)
    h_part = (
        loads[inner_count]
        - matmul(interior[inner_count - 1], coup_last)
        - matmul(got_first, coup_sep.T)
    )
    for level_index in range(levels):
        distance = 1 << level_index
        b_full, c_full = (
            lax.all_gather(b_part, "col", axis=1, tiled=True),
            lax.all_gather(c_part, "col", axis=1, tiled=True),
        )
        inverse = invert(b_full)
        coupling_rows = lax.dynamic_slice_in_dim(c_full, col_start, col_width, 0)
        solved_cols = matmul(inverse, c_part)
        solved_loads = matmul(h_part, inverse.T)
        below_blocks, below_loads = passed_along(
            (matmul(c_full.T, solved_cols), matmul(solved_loads, c_full)), "chain", distance
        )
        far_inverse, far_cols, far_loads = passed_along(
            (inverse, solved_cols, solved_loads), "chain", -distance
        )
        b_part = b_part - below_blocks - matmul(c_full, matmul(far_inverse, coupling_rows.T))
        c_part = -matmul(c_full, far_cols)
        h_part = h_part - below_loads - matmul(far_loads, c_full.T)
    b_final = lax.all_gather(b_part, "col", axis=1, tiled=True)
    separator = jax.scipy.linalg.cho_solve((jnp.linalg.cholesky(b_final), True), h_part.T).T
    carried = passed_along(matmul(separator, coup_sep), "chain", 1)
    adjusted = loads[:inner_count]
    adjusted = adjusted.at[0].add(-carried)
    adjusted = adjusted.at[inner_count - 1].add(-matmul(separator, coup_last.T))
    solved_inner = interior_solve(adjusted, inverses, products, inner_coups)
    return jnp.swapaxes(jnp.concatenate([solved_inner, separator[None]], axis=0), 0, 1)


def solution(mesh):
    in_specs = (P("chain", "col", None), P("chain", "col", None), P("col", "chain", None))
    out_specs = P("col", "chain", None)
    return jax.shard_map(
        per_device, mesh=mesh, in_specs=in_specs, out_specs=out_specs, check_vma=False
    )
```

profile of v0, /device:TPU:1, one launch (start us, length us, event | category | flops | bytes accessed | tf_op | source)
XLA Modules:
  0.0 920.7 jit_solution(14875295477138087786)
XLA Ops:
  1.0 12.3 %all_gather.45 = f32[2,256,256]{2,0,1:T(2,128)S(1)} all-gather(f32[2,64,256]{2,0,1:T(2,128)S(1)} %copy.26), channel_id=1, replica_groups=mesh['chain'=64,'col'=4] {'col'}, dimensions={1}, use_global_device_ids=true | all-gather | bytes 655360 | tf_op jit(solution)/shard_map/all_gather | solution.py:53
  14.0 11.7 %cholesky.424 = f32[128,128]{1,0:T(8,128)S(1)} custom-call(f32[128,128]{1,0:T(8,128)S(1)} %cholesky.726), custom_call_target="Cholesky" | custom-call | tf_op jit(solution)/shard_map/jit(cholesky)/cholesky | solution.py:20
  36.1 11.7 %cholesky.441 = f32[128,128]{1,0:T(8,128)S(1)} custom-call(f32[128,128]{1,0:T(8,128)S(1)} %convolution_subtract_fusion.24), custom_call_target="Cholesky" | custom-call | tf_op jit(solution)/shard_map/jit(cholesky)/cholesky | solution.py:20
  53.8 19.7 %custom-call.37 = f32[2,128,128]{1,2,0:T(8,128)S(1)} custom-call(f32[2,128,128]{2,1,0:T(8,128)S(1)} %get-tuple-element.218), custom_call_target="InvertDiagBlocksLowerTriangular" | custom-call | tf_op jit(solution)/shard_map/jit(_cho_solve)/triangular_solve | solution.py:22
  89.3 11.7 %cholesky.458 = f32[128,128]{1,0:T(8,128)S(1)} custom-call(f32[128,128]{1,0:T(8,128)S(1)} %cholesky.729), custom_call_target="Cholesky" | custom-call | tf_op jit(solution)/shard_map/while/body/eval_jaxpr/jit(cholesky)/cholesky | solution.py:20
  111.4 11.7 %cholesky.475 = f32[128,128]{1,0:T(8,128)S(1)} custom-call(f32[128,128]{1,0:T(8,128)S(1)} %convolution_subtract_fusion.23), custom_call_target="Cholesky" | custom-call | tf_op jit(solution)/shard_map/while/body/eval_jaxpr/jit(cholesky)/cholesky | solution.py:20
  129.9 19.7 %custom-call.39 = f32[2,128,128]{1,2,0:T(8,128)S(1)} custom-call(f32[2,128,128]{2,1,0:T(8,128)S(1)} %get-tuple-element.219), custom_call_target="InvertDiagBlocksLowerTriangular" | custom-call | tf_op jit(solution)/shard_map/while/body/eval_jaxpr/jit(_cho_solve)/triangular_solve | solution.py:22
  198.0 11.7 %cholesky.492 = f32[128,128]{1,0:T(8,128)S(1)} custom-call(f32[128,128]{1,0:T(8,128)S(1)} %cholesky.732), custom_call_target="Cholesky" | custom-call | tf_op jit(solution)/shard_map/jit(cholesky)/cholesky | solution.py:20
  220.1 11.7 %cholesky.509 = f32[128,128]{1,0:T(8,128)S(1)} custom-call(f32[128,128]{1,0:T(8,128)S(1)} %convolution_subtract_fusion.22), custom_call_target="Cholesky" | custom-call | tf_op jit(solution)/shard_map/jit(cholesky)/cholesky | solution.py:20
  239.5 19.7 %custom-call.41 = f32[2,128,128]{1,2,0:T(8,128)S(1)} custom-call(f32[2,128,128]{2,1,0:T(8,128)S(1)} %get-tuple-element.220), custom_call_target="InvertDiagBlocksLowerTriangular" | custom-call | tf_op jit(solution)/shard_map/jit(_cho_solve)/triangular_solve | solution.py:22
  301.1 11.7 %cholesky.526 = f32[128,128]{1,0:T(8,128)S(1)} custom-call(f32[128,128]{1,0:T(8,128)S(1)} %cholesky.735), custom_call_target="Cholesky" | custom-call | tf_op jit(solution)/shard_map/jit(cholesky)/cholesky | solution.py:20
  323.2 11.7 %cholesky.543 = f32[128,128]{1,0:T(8,128)S(1)} custom-call(f32[128,128]{1,0:T(8,128)S(1)} %convolution_subtract_fusion.21), custom_call_target="Cholesky" | custom-call | tf_op jit(solution)/shard_map/jit(cholesky)/cholesky | solution.py:20
  343.3 19.7 %custom-call.43 = f32[2,128,128]{1,2,0:T(8,128)S(1)} custom-call(f32[2,128,128]{2,1,0:T(8,128)S(1)} %get-tuple-element.221), custom_call_target="InvertDiagBlocksLowerTriangular" | custom-call | tf_op jit(solution)/shard_map/jit(_cho_solve)/triangular_solve | solution.py:22
  423.0 11.7 %cholesky.577 = f32[128,128]{1,0:T(8,128)S(1)} custom-call(f32[128,128]{1,0:T(8,128)S(1)} %convolution_subtract_fusion.20), custom_call_target="Cholesky" | custom-call | tf_op jit(solution)/shard_map/jit(cholesky)/cholesky | solution.py:20
  441.9 19.7 %custom-call.45 = f32[2,128,128]{1,2,0:T(8,128)S(1)} custom-call(f32[2,128,128]{2,1,0:T(8,128)S(1)} %get-tuple-element.222), custom_call_target="InvertDiagBlocksLowerTriangular" | custom-call | tf_op jit(solution)/shard_map/jit(_cho_solve)/triangular_solve | solution.py:22
  531.7 11.7 %cholesky.611 = f32[128,128]{1,0:T(8,128)S(1)} custom-call(f32[128,128]{1,0:T(8,128)S(1)} %convolution_subtract_fusion.19), custom_call_target="Cholesky" | custom-call | tf_op jit(solution)/shard_map/jit(cholesky)/cholesky | solution.py:20
  551.5 19.7 %custom-call.47 = f32[2,128,128]{1,2,0:T(8,128)S(1)} custom-call(f32[2,128,128]{2,1,0:T(8,128)S(1)} %get-tuple-element.223), custom_call_target="InvertDiagBlocksLowerTriangular" | custom-call | tf_op jit(solution)/shard_map/jit(_cho_solve)/triangular_solve | solution.py:22
  634.2 11.7 %cholesky.645 = f32[128,128]{1,0:T(8,128)S(1)} custom-call(f32[128,128]{1,0:T(8,128)S(1)} %convolution_subtract_fusion.18), custom_call_target="Cholesky" | custom-call | tf_op jit(solution)/shard_map/jit(cholesky)/cholesky | solution.py:20
  653.3 19.7 %custom-call.49 = f32[2,128,128]{1,2,0:T(8,128)S(1)} custom-call(f32[2,128,128]{2,1,0:T(8,128)S(1)} %get-tuple-element.224), custom_call_target="InvertDiagBlocksLowerTriangular" | custom-call | tf_op jit(solution)/shard_map/jit(_cho_solve)/triangular_solve | solution.py:22
  741.6 11.7 %cholesky.679 = f32[128,128]{1,0:T(8,128)S(1)} custom-call(f32[128,128]{1,0:T(8,128)S(1)} %convolution_subtract_fusion.17), custom_call_target="Cholesky" | custom-call | tf_op jit(solution)/shard_map/jit(cholesky)/cholesky | solution.py:20
  762.0 19.7 %custom-call.51 = f32[2,128,128]{1,2,0:T(8,128)S(1)} custom-call(f32[2,128,128]{2,1,0:T(8,128)S(1)} %get-tuple-element.225), custom_call_target="InvertDiagBlocksLowerTriangular" | custom-call | tf_op jit(solution)/shard_map/jit(_cho_solve)/triangular_solve | solution.py:22
  839.8 11.7 %cholesky.713 = f32[128,128]{1,0:T(8,128)S(1)} custom-call(f32[128,128]{1,0:T(8,128)S(1)} %convolution_subtract_fusion.16), custom_call_target="Cholesky" | custom-call | tf_op jit(solution)/shard_map/jit(cholesky)/cholesky | solution.py:119
  858.9 19.7 %custom-call.20 = f32[2,128,128]{1,2,0:T(8,128)S(1)} custom-call(f32[2,128,128]{2,1,0:T(8,128)S(1)} %get-tuple-element.175), custom_call_target="InvertDiagBlocksLowerTriangular" | custom-call | tf_op jit(solution)/shard_map/jit(_cho_solve)/triangular_solve | solution.py:119
  880.2 36.1 %collective-permute-start.32 = (f32[16,256]{1,0:T(8,128)S(1)}, f32[16,256]{1,0:T(8,128)S(1)}, u32[]{:S(2)}, u32[]{:S(2)}) collective-permute-start(f32[16,256]{1,0:T(8,128)S(1)} %fusion.28), channel_id=1, source_target_pairs={{0,4},{4,8},{8,12},{12,16},{16,20},{20,24},{24,28},{28,32},{32,36}... | collective-permute-start | bytes 49160 | tf_op jit(solution)/shard_map/ppermute | solution.py:12
  (480 shorter events, 570.4 us)
Async XLA Ops:
  154.4 16.6 %collective-permute-start.19 = (f32[16,256]{1,0:T(8,128)}, f32[16,256]{1,0:T(8,128)S(1)}, u32[]{:S(2)}, u32[]{:S(2)}) collective-permute-start(f32[16,256]{1,0:T(8,128)} %convolution_subtract_fusion.29), channel_id=1, source_target_pairs={{4,0},{8,4},{12,8},{16,12},{20,16},{24,20},{28,24},{32,28},{36,32}... | collective-permute-start | bytes 49160 | tf_op jit(solution)/shard_map/ppermute | solution.py:12
  165.0 19.6 %collective-permute-start = (f32[256,256]{1,0:T(8,128)}, f32[256,256]{1,0:T(8,128)S(1)}, u32[]{:S(2)}, u32[]{:S(2)}) collective-permute-start(f32[256,256]{1,0:T(8,128)} %convolution_add_fusion), channel_id=1, source_target_pairs={{4,0},{8,4},{12,8},{16,12},{20,16},{24,20},{28,24},{32,28},{36,32}... | collective-permute-start | bytes 786440 | tf_op jit(solution)/shard_map/ppermute | solution.py:12
  261.6 17.7 %collective-permute-start.21 = (f32[16,256]{1,0:T(8,128)S(1)}, f32[16,256]{1,0:T(8,128)S(1)}, u32[]{:S(2)}, u32[]{:S(2)}) collective-permute-start(f32[16,256]{1,0:T(8,128)S(1)} %fusion.228), channel_id=1, source_target_pairs={{4,0},{8,4},{12,8},{16,12},{20,16},{24,20},{28,24},{32,28},{36,32}... | collective-permute-start | bytes 49160 | tf_op jit(solution)/shard_map/ppermute | solution.py:12
  268.4 97.4 %collective-permute-start.20 = (f32[16,256]{1,0:T(8,128)}, f32[16,256]{1,0:T(8,128)S(1)}, u32[]{:S(2)}, u32[]{:S(2)}) collective-permute-start(f32[16,256]{1,0:T(8,128)} %fusion.247), channel_id=1, source_target_pairs={{0,4},{4,8},{8,12},{12,16},{16,20},{20,24},{24,28},{28,32},{32,36}... | collective-permute-start | bytes 49160 | tf_op jit(solution)/shard_map/ppermute | solution.py:12
  273.7 16.6 %collective-permute-start.3 = (f32[256,256]{1,0:T(8,128)S(1)}, f32[256,256]{1,0:T(8,128)S(1)}, u32[]{:S(2)}, u32[]{:S(2)}) collective-permute-start(f32[256,256]{1,0:T(8,128)S(1)} %pad_maximum_fusion.3), channel_id=1, source_target_pairs={{4,0},{8,4},{12,8},{16,12},{20,16},{24,20},{28,24},{32,28},{36,32}... | collective-permute-start | bytes 786440 | tf_op jit(solution)/shard_map/ppermute | solution.py:12
  275.6 15.2 %collective-permute-start.2 = (f32[256,64]{0,1:T(8,128)S(1)}, f32[256,64]{0,1:T(8,128)S(1)}, u32[]{:S(2)}, u32[]{:S(2)}) collective-permute-start(f32[256,64]{0,1:T(8,128)S(1)} %fusion.241), channel_id=1, source_target_pairs={{0,4},{4,8},{8,12},{12,16},{16,20},{20,24},{24,28},{28,32},{32,36}... | collective-permute-start | bytes 196616 | tf_op jit(solution)/shard_map/ppermute | solution.py:12
  374.0 15.9 %collective-permute-start.6 = (f32[256,256]{1,0:T(8,128)S(1)}, f32[256,256]{1,0:T(8,128)S(1)}, u32[]{:S(2)}, u32[]{:S(2)}) collective-permute-start(f32[256,256]{1,0:T(8,128)S(1)} %pad_maximum_fusion.4), channel_id=1, source_target_pairs={{8,0},{12,4},{16,8},{20,12},{24,16},{28,20},{32,24},{36,28},{40,32... | collective-permute-start | bytes 786440 | tf_op jit(solution)/shard_map/ppermute | solution.py:12
  464.5 23.0 %collective-permute-start.25 = (f32[16,256]{1,0:T(8,128)S(1)}, f32[16,256]{1,0:T(8,128)S(1)}, u32[]{:S(2)}, u32[]{:S(2)}) collective-permute-start(f32[16,256]{1,0:T(8,128)S(1)} %fusion.225), channel_id=1, source_target_pairs={{16,0},{20,4},{24,8},{28,12},{32,16},{36,20},{40,24},{44,28},{48,3... | collective-permute-start | bytes 49160 | tf_op jit(solution)/shard_map/ppermute | solution.py:12
  467.2 20.6 %collective-permute-start.10 = (f32[256,64]{0,1:T(8,128)S(1)}, f32[256,64]{0,1:T(8,128)S(1)}, u32[]{:S(2)}, u32[]{:S(2)}) collective-permute-start(f32[256,64]{0,1:T(8,128)S(1)} %fusion.226), channel_id=1, source_target_pairs={{16,0},{20,4},{24,8},{28,12},{32,16},{36,20},{40,24},{44,28},{48,3... | collective-permute-start | bytes 196616 | tf_op jit(solution)/shard_map/ppermute | solution.py:12
  468.5 105.4 %collective-permute-start.24 = (f32[16,256]{1,0:T(8,128)}, f32[16,256]{1,0:T(8,128)S(1)}, u32[]{:S(2)}, u32[]{:S(2)}) collective-permute-start(f32[16,256]{1,0:T(8,128)} %fusion.250), channel_id=1, source_target_pairs={{0,16},{4,20},{8,24},{12,28},{16,32},{20,36},{24,40},{28,44},{32,4... | collective-permute-start | bytes 49160 | tf_op jit(solution)/shard_map/ppermute | solution.py:12
  479.5 18.7 %collective-permute-start.9 = (f32[256,256]{1,0:T(8,128)S(1)}, f32[256,256]{1,0:T(8,128)S(1)}, u32[]{:S(2)}, u32[]{:S(2)}) collective-permute-start(f32[256,256]{1,0:T(8,128)S(1)} %pad_maximum_fusion.5), channel_id=1, source_target_pairs={{16,0},{20,4},{24,8},{28,12},{32,16},{36,20},{40,24},{44,28},{48,3... | collective-permute-start | bytes 786440 | tf_op jit(solution)/shard_map/ppermute | solution.py:12
  480.8 17.8 %collective-permute-start.8 = (f32[256,64]{0,1:T(8,128)S(1)}, f32[256,64]{0,1:T(8,128)S(1)}, u32[]{:S(2)}, u32[]{:S(2)}) collective-permute-start(f32[256,64]{0,1:T(8,128)S(1)} %fusion.243), channel_id=1, source_target_pairs={{0,16},{4,20},{8,24},{12,28},{16,32},{20,36},{24,40},{28,44},{32,4... | collective-permute-start | bytes 196616 | tf_op jit(solution)/shard_map/ppermute | solution.py:12
  574.5 16.6 %collective-permute-start.27 = (f32[16,256]{1,0:T(8,128)S(1)}, f32[16,256]{1,0:T(8,128)S(1)}, u32[]{:S(2)}, u32[]{:S(2)}) collective-permute-start(f32[16,256]{1,0:T(8,128)S(1)} %fusion.210), channel_id=1, source_target_pairs={{32,0},{36,4},{40,8},{44,12},{48,16},{52,20},{56,24},{60,28},{64,3... | collective-permute-start | bytes 49160 | tf_op jit(solution)/shard_map/ppermute | solution.py:12
  576.0 15.1 %collective-permute-start.26 = (f32[16,256]{1,0:T(8,128)S(1)}, f32[16,256]{1,0:T(8,128)S(1)}, u32[]{:S(2)}, u32[]{:S(2)}) collective-permute-start(f32[16,256]{1,0:T(8,128)S(1)} %fusion.252), channel_id=1, source_target_pairs={{0,32},{4,36},{8,40},{12,44},{16,48},{20,52},{24,56},{28,60},{32,6... | collective-permute-start | bytes 49160 | tf_op jit(solution)/shard_map/ppermute | solution.py:12
  584.6 16.5 %collective-permute-start.12 = (f32[256,256]{1,0:T(8,128)S(1)}, f32[256,256]{1,0:T(8,128)S(1)}, u32[]{:S(2)}, u32[]{:S(2)}) collective-permute-start(f32[256,256]{1,0:T(8,128)S(1)} %pad_maximum_fusion.6), channel_id=1, source_target_pairs={{32,0},{36,4},{40,8},{44,12},{48,16},{52,20},{56,24},{60,28},{64,3... | collective-permute-start | bytes 786440 | tf_op jit(solution)/shard_map/ppermute | solution.py:12
  585.9 15.6 %collective-permute-start.11 = (f32[256,64]{0,1:T(8,128)S(1)}, f32[256,64]{0,1:T(8,128)S(1)}, u32[]{:S(2)}, u32[]{:S(2)}) collective-permute-start(f32[256,64]{0,1:T(8,128)S(1)} %fusion.244), channel_id=1, source_target_pairs={{0,32},{4,36},{8,40},{12,44},{16,48},{20,52},{24,56},{28,60},{32,6... | collective-permute-start | bytes 196616 | tf_op jit(solution)/shard_map/ppermute | solution.py:12
  676.0 22.1 %collective-permute-start.29 = (f32[16,256]{1,0:T(8,128)S(1)}, f32[16,256]{1,0:T(8,128)S(1)}, u32[]{:S(2)}, u32[]{:S(2)}) collective-permute-start(f32[16,256]{1,0:T(8,128)S(1)} %fusion.222), channel_id=1, source_target_pairs={{64,0},{68,4},{72,8},{76,12},{80,16},{84,20},{88,24},{92,28},{96,3... | collective-permute-start | bytes 49160 | tf_op jit(solution)/shard_map/ppermute | solution.py:12
  678.7 19.6 %collective-permute-start.16 = (f32[256,64]{0,1:T(8,128)S(1)}, f32[256,64]{0,1:T(8,128)S(1)}, u32[]{:S(2)}, u32[]{:S(2)}) collective-permute-start(f32[256,64]{0,1:T(8,128)S(1)} %fusion.223), channel_id=1, source_target_pairs={{64,0},{68,4},{72,8},{76,12},{80,16},{84,20},{88,24},{92,28},{96,3... | collective-permute-start | bytes 196616 | tf_op jit(solution)/shard_map/ppermute | solution.py:12
  680.0 104.5 %collective-permute-start.28 = (f32[16,256]{1,0:T(8,128)}, f32[16,256]{1,0:T(8,128)S(1)}, u32[]{:S(2)}, u32[]{:S(2)}) collective-permute-start(f32[16,256]{1,0:T(8,128)} %fusion.253), channel_id=1, source_target_pairs={{0,64},{4,68},{8,72},{12,76},{16,80},{20,84},{24,88},{28,92},{32,9... | collective-permute-start | bytes 49160 | tf_op jit(solution)/shard_map/ppermute | solution.py:12
  690.1 18.5 %collective-permute-start.15 = (f32[256,256]{1,0:T(8,128)S(1)}, f32[256,256]{1,0:T(8,128)S(1)}, u32[]{:S(2)}, u32[]{:S(2)}) collective-permute-start(f32[256,256]{1,0:T(8,128)S(1)} %pad_maximum_fusion.7), channel_id=1, source_target_pairs={{64,0},{68,4},{72,8},{76,12},{80,16},{84,20},{88,24},{92,28},{96,3... | collective-permute-start | bytes 786440 | tf_op jit(solution)/shard_map/ppermute | solution.py:12
  691.4 17.6 %collective-permute-start.14 = (f32[256,64]{0,1:T(8,128)S(1)}, f32[256,64]{0,1:T(8,128)S(1)}, u32[]{:S(2)}, u32[]{:S(2)}) collective-permute-start(f32[256,64]{0,1:T(8,128)S(1)} %fusion.245), channel_id=1, source_target_pairs={{0,64},{4,68},{8,72},{12,76},{16,80},{20,84},{24,88},{28,92},{32,9... | collective-permute-start | bytes 196616 | tf_op jit(solution)/shard_map/ppermute | solution.py:12
  784.7 19.2 %collective-permute-start.31 = (f32[16,256]{1,0:T(8,128)S(1)}, f32[16,256]{1,0:T(8,128)S(1)}, u32[]{:S(2)}, u32[]{:S(2)}) collective-permute-start(f32[16,256]{1,0:T(8,128)S(1)} %fusion.211), channel_id=1, source_target_pairs={{128,0},{132,4},{136,8},{140,12},{144,16},{148,20},{152,24},{156,2... | collective-permute-start | bytes 49160 | tf_op jit(solution)/shard_map/ppermute | solution.py:12
  786.3 17.6 %collective-permute-start.30 = (f32[16,256]{1,0:T(8,128)S(1)}, f32[16,256]{1,0:T(8,128)S(1)}, u32[]{:S(2)}, u32[]{:S(2)}) collective-permute-start(f32[16,256]{1,0:T(8,128)S(1)} %fusion.255), channel_id=1, source_target_pairs={{0,128},{4,132},{8,136},{12,140},{16,144},{20,148},{24,152},{28,15... | collective-permute-start | bytes 49160 | tf_op jit(solution)/shard_map/ppermute | solution.py:12
  880.2 36.9 %collective-permute-start.32 = (f32[16,256]{1,0:T(8,128)S(1)}, f32[16,256]{1,0:T(8,128)S(1)}, u32[]{:S(2)}, u32[]{:S(2)}) collective-permute-start(f32[16,256]{1,0:T(8,128)S(1)} %fusion.28), channel_id=1, source_target_pairs={{0,4},{4,8},{8,12},{12,16},{16,20},{20,24},{24,28},{28,32},{32,36}... | collective-permute-start | bytes 49160 | tf_op jit(solution)/shard_map/ppermute | solution.py:12
  (41 other events, 199.7 us)
where the time goes:
time: 934 us; the launch traced here: 921 us
  other arithmetic  490 us (52%)
  starting transfers between devices  155 us (17%)
  blocking collectives  148 us (16%)
  local copies, waits for them, and re-layouts  56.2 us (6%)
  matrix products  47.9 us (5%)
  between operations  13.9 us (1%)
    another operation x55, other arithmetic, invert(): lower_factor = jnp.linalg.cholesky(matrix)  276 us
    another operation x23, other arithmetic, invert(): return jax.scipy.linalg.cho_solve((lower_factor, True), identity)  158 us
    ppermute x33, starting transfers between devices, passed_along(): return lax.ppermute(shard, axis, pairs)  155 us
    all_gather x6, blocking collectives, per_device(): lax.all_gather(b_part, 'col', axis=1, tiled=True)  57.8 us
    all_gather x6, blocking collectives, per_device(): lax.all_gather(c_part, 'col', axis=1, tiled=True)  57.5 us
    another operation x58, local copies, waits for them, and re-layouts, invert(): return jax.scipy.linalg.cho_solve((lower_factor, True), identity)  35.5 us
    another operation x7, other arithmetic, per_device(): jnp.linalg.cholesky(b_final)  34.6 us
    dot_general x71, matrix products, matmul(): return jnp.dot(first_factor, second_factor, precision=finest)  28.7 us
  transfers between devices with their start and end apart: 33, of which 4 were waited for; matrix products, arithmetic and copies ran while one was open for 22% of the time, Pallas kernels for 0%

commit v1 on v0

v1 whole, which is shorter than its diff:
```python
import functools

import jax
import jax.numpy as jnp
from jax import lax
from jax.experimental import pallas as pl
from jax.experimental.pallas import tpu as pltpu
from jax.sharding import PartitionSpec as P

MESH = pl.DeviceIdType.MESH
PIVOTS = 32
SUB = 8


def dot_nn(a, b):
    return lax.dot_general(
        a, b, (((1,), (0,)), ((), ())),
        precision=lax.Precision.HIGHEST, preferred_element_type=jnp.float32,
    )


def dot_nt(a, b):
    return lax.dot_general(
        a, b, (((1,), (1,)), ((), ())),
        precision=lax.Precision.HIGHEST, preferred_element_type=jnp.float32,
    )


def sweep_panel(block, panel):
    count = len(block)
    ids = lax.broadcasted_iota(jnp.int32, block[0].shape, 0)
    ids_wide = lax.broadcasted_iota(jnp.int32, panel[0].shape, 0)
    reps = panel[0].shape[1] // block[0].shape[1]

    def wide(v):
        return jnp.concatenate([v] * reps, axis=1)

    for at in range(count):
        cols = [
            [jnp.broadcast_to(g[:, at * SUB + j : at * SUB + j + 1], block[0].shape) for g in block]
            for j in range(SUB)
        ]
        for s in range(SUB):
            pivot_col = cols[s]
            inv_pivot = 1.0 / jnp.broadcast_to(pivot_col[at][s : s + 1, :], block[0].shape)
            factors = [c * inv_pivot for c in pivot_col]
            factors_wide = [wide(f) for f in factors]
            inv_wide = wide(inv_pivot)

            def eliminated(groups, facs, inv, hit):
                row = jnp.broadcast_to(groups[at][s : s + 1, :], groups[0].shape)
                out = [g - f * row for g, f in zip(groups, facs)]
                out[at] = jnp.where(hit, inv * row, out[at])
                return out

            for j in range(s + 1, SUB):
                cols[j] = eliminated(cols[j], factors, inv_pivot, ids == s)
            if at < count - 1:
                block = eliminated(block, factors, inv_pivot, ids == s)
            panel = eliminated(panel, factors_wide, inv_wide, ids_wide == s)
    return panel


def invert_in_place(ref, hook=None):
    size = ref.shape[0]
    lane = lax.broadcasted_iota(jnp.int32, (PIVOTS, size), 1)
    row = lax.broadcasted_iota(jnp.int32, (PIVOTS, size), 0)
    lane_low = lax.broadcasted_iota(jnp.int32, (size - PIVOTS, size), 1)
    unit = (lane == row).astype(jnp.float32)

    def step(i, carry):
        top = ref[0:PIVOTS, :]
        low = ref[PIVOTS:, :]
        start = jnp.where(lane < PIVOTS, unit, top)
        groups = range(0, PIVOTS, SUB)
        swept = sweep_panel(
            [top[g : g + SUB, 0:128] for g in groups], [start[g : g + SUB, :] for g in groups]
        )
        swept = jnp.concatenate(swept, axis=0)
        rest = jnp.where(lane_low < PIVOTS, 0.0, low) - dot_nn(low[:, 0:PIVOTS], swept)
        ref[0 : size - PIVOTS, :] = pltpu.roll(rest, size - PIVOTS, 1)
        ref[size - PIVOTS :, :] = pltpu.roll(swept, size - PIVOTS, 1)
        if hook is not None:
            @pl.when(i == 2)
            def _():
                hook()
        return carry

    lax.fori_loop(0, size // PIVOTS, step, 0)


def kernel(
    n, m, levels,
    diag, coup, loads, out,
    gath, inv0, inv1, work, c0t, f1, g1, wide0, wide1, hq, bq, dnb, dnh,
    send_b, send_fg, send_h, got_b, got_h, xb, xfg, sol, got_sol,
    s_first_send, s_first_recv, s_c2, s_sol,
    s_send, s_x_send, r_b, r_fg, r_h, r_xb, r_xfg,
):
    k = lax.axis_index("chain")
    x = lax.axis_index("col")
    q = diag.shape[1]
    size = diag.shape[2]
    nrhs = loads.shape[1]
    own = pl.ds(pl.multiple_of(x * q, q), q)
    has_up = k + 1 < n
    has_low = k >= 1

    def place(p):
        return pl.ds(pl.multiple_of(lax.rem(x + m - p, m) * q, q), q)

    def copy(src, dst, send, recv, chain, col):
        return pltpu.make_async_remote_copy(
            src_ref=src, dst_ref=dst, send_sem=send, recv_sem=recv,
            device_id=(chain, col), device_id_type=MESH,
        )

    def zero(ref):
        ref[...] = jnp.zeros(ref.shape, jnp.float32)

    @pl.when(jnp.logical_not(has_low))
    def _():
        zero(gath.at[4, own])

    def fill(e, d):
        @pl.when(k - d < 0)
        def _():
            zero(got_b.at[e, 0])
            zero(got_h.at[e, 0])
            zero(xfg.at[e, 0, own])

        @pl.when(k + d >= n)
        def _():
            zero(got_b.at[e, 1])
            zero(got_h.at[e, 1])
            zero(xfg.at[e, 1, own])

        return d * 2

    lax.fori_loop(1, levels + 1, fill, 1)

    @pl.when(jnp.logical_not(has_up))
    def _():
        zero(got_b.at[0, 1])
        zero(got_h.at[0, 1])
        zero(xfg.at[0, 1, own])

    barrier = pltpu.get_barrier_semaphore()
    partners = m - 1
    for p in range(1, m):
        pl.semaphore_signal(barrier, inc=1, device_id=(k, lax.rem(x + p, m)), device_id_type=MESH)
    for level in range(levels):
        d = 1 << level
        for cond, other in ((k + d < n, k + d), (k - d >= 0, k - d)):
            @pl.when(cond)
            def _():
                pl.semaphore_signal(barrier, inc=1, device_id=(other, x), device_id_type=MESH)
            partners = partners + cond.astype(jnp.int32)
    pl.semaphore_wait(barrier, partners)

    def first(i, src, p):
        return copy(src, gath.at[i, own], s_first_send.at[i, p - 1], s_first_recv.at[i, p - 1], k, lax.rem(x + p, m))

    def first_wait(i):
        for p in range(1, m):
            copy(
                gath.at[i, place(p)], gath.at[i, place(p)], s_first_send.at[i, p - 1], s_first_recv.at[i, p - 1],
                k, lax.rem(x + p, m),
            ).wait_recv()

    sources = (diag.at[0], coup.at[0], diag.at[1], coup.at[1], gath.at[4, own])
    for p in range(1, m):
        first(0, sources[0], p).start()

    def c2_copy():
        return copy(coup.at[2], gath.at[4, own], s_c2.at[0], s_c2.at[1], lax.rem(k + 1, n), x)

    @pl.when(has_up)
    def _():
        c2_copy().start()

    for i in range(1, 4):
        for p in range(1, m):
            first(i, sources[i], p).start()
    for i in range(4):
        gath[i, own] = sources[i][...]
    first_wait(0)

    inv0[...] = gath[0]

    def forward_c2():
        @pl.when(has_low)
        def _():
            c2_copy().wait_recv()

        for p in range(1, m):
            first(4, sources[4], p).start()

    invert_in_place(inv0, forward_c2)
    first_wait(1)
    first_wait(2)
    first_wait(4)
    c0 = gath[1]
    f0 = gath[4]
    inverse = inv0[...]
    c0t[...] = c0.T
    wide0[...] = dot_nn(f0, inverse)
    wide1[...] = dot_nn(c0t[...], inverse)
    f1[...] = -dot_nn(wide0[...], c0)
    inv1[...] = gath[2] - dot_nn(wide1[...], c0)
    wh0 = dot_nn(loads[0], inverse)
    hq[1] = loads[1] - dot_nn(wh0, c0)
    dnb[...] = dot_nt(wide0[own], f0)
    dnh[...] = dot_nt(wh0, f0)

    invert_in_place(inv1)
    first_wait(3)
    g1[...] = gath[3].T

    def chain_send(e, kind, side, d):
        other = lax.rem(k + d, n) if side == 0 else lax.rem(k - d + n, n)
        src, dst, recv = (
            (send_b.at[side], got_b.at[e, side], r_b),
            (send_fg.at[side], xfg.at[e, side, own], r_fg),
            (send_h.at[side], got_h.at[e, side], r_h),
        )[kind]
        return copy(src, dst, s_send.at[kind, side], recv.at[e, side], other, x)

    def spread(e, p):
        return copy(
            xb.at[e, own], xb.at[e, own], s_x_send.at[0, p - 1], r_xb.at[e, p - 1], k, lax.rem(x + p, m)
        )

    def spread_fg(e, p):
        return copy(
            xfg.at[e, :, own], xfg.at[e, :, own], s_x_send.at[1, p - 1], r_xfg.at[e, p - 1], k, lax.rem(x + p, m)
        )

    def spread_wait(e, p):
        copy(
            xb.at[e, place(p)], xb.at[e, place(p)], s_x_send.at[0, p - 1], r_xb.at[e, p - 1], k, lax.rem(x + p, m)
        ).wait_recv()

    def spread_fg_wait(e, p):
        copy(
            xfg.at[e, :, place(p)], xfg.at[e, :, place(p)], s_x_send.at[1, p - 1], r_xfg.at[e, p - 1],
            k, lax.rem(x + p, m),
        ).wait_recv()

    stacked = jnp.concatenate([f1[own], g1[own], hq[1]], axis=0)
    w = dot_nn(stacked, inv1[...])
    w_f, w_g, w_h = w[0:q], w[q : 2 * q], w[2 * q :]
    send_b[1] = dnb[...] + dot_nt(w_f, f1[...])
    @pl.when(has_low)
    def _():
        chain_send(0, 0, 1, 1).start()

    send_fg[1] = -dot_nt(w_g, f1[...])
    send_h[1] = dnh[...] + dot_nt(w_h, f1[...])
    @pl.when(has_low)
    def _():
        chain_send(0, 1, 1, 1).start()
        chain_send(0, 2, 1, 1).start()

    own_terms = dot_nt(w, g1[...])
    xfg[0, 0, own] = -own_terms[0:q]
    hq[2] = loads[2] - own_terms[2 * q :]
    local_b = diag[2] - own_terms[q : 2 * q]

    @pl.when(has_up)
    def _():
        chain_send(0, 0, 1, 1).wait_recv()

    bq[...] = local_b - got_b[0, 1]
    xb[0, own] = bq[...]
    for p in range(1, m):
        spread(0, p).start()

    @pl.when(has_low)
    def _():
        for kind in range(3):
            chain_send(0, kind, 1, 1).wait_send()

    zero(got_h.at[0, 0])

    def level(l, half):
        below = jnp.logical_and(l >= 1, k - half >= 0)
        above = k + half < n
        full = jnp.where(l == 0, 1, 2 * half)
        up_ok = k + full < n
        low_ok = k - full >= 0
        more = l < levels

        for p in range(1, m):
            spread_wait(l, p)
        work[...] = xb[l]

        def forward_fg():
            @pl.when(jnp.logical_and(above, more))
            def _():
                chain_send(l, 1, 1, half).wait_recv()

            @pl.when(jnp.logical_and(below, more))
            def _():
                chain_send(l, 1, 0, half).wait_recv()

            @pl.when(more)
            def _():
                for p in range(1, m):
                    spread_fg(l, p).start()

        invert_in_place(work, forward_fg)
        for p in range(1, m):
            spread(l, p).wait_send()

        @pl.when(above)
        def _():
            chain_send(l, 2, 1, half).wait_recv()

        @pl.when(below)
        def _():
            chain_send(l, 2, 0, half).wait_recv()

        hq[2] = hq[2] - got_h[l, 0] - got_h[l, 1]

        @pl.when(more)
        def _():
            for p in range(1, m):
                spread_fg_wait(l, p)
            stacked = jnp.concatenate([xfg[l, 0, own], xfg[l, 1, own], hq[2]], axis=0)
            w = dot_nn(stacked, work[...])
            send_b[1] = dot_nt(w[0:q], xfg[l, 0])
            send_b[0] = dot_nt(w[q : 2 * q], xfg[l, 1])

            @pl.when(low_ok)
            def _():
                chain_send(l + 1, 0, 1, full).start()

            @pl.when(up_ok)
            def _():
                chain_send(l + 1, 0, 0, full).start()

            to_low = dot_nt(w[q:], xfg[l, 0])
            send_fg[1] = -to_low[0:q]
            send_h[1] = to_low[q:]

            @pl.when(low_ok)
            def _():
                chain_send(l + 1, 2, 1, full).start()

            to_up_f = dot_nt(w[0:q], xfg[l, 1])
            send_fg[0] = -to_up_f
            send_h[0] = dot_nt(w[2 * q :], xfg[l, 1])

            @pl.when(up_ok)
            def _():
                chain_send(l + 1, 2, 0, full).start()

            @pl.when(jnp.logical_and(low_ok, l + 1 < levels))
            def _():
                chain_send(l + 1, 1, 1, full).start()

            @pl.when(jnp.logical_and(up_ok, l + 1 < levels))
            def _():
                chain_send(l + 1, 1, 0, full).start()

            @pl.when(up_ok)
            def _():
                chain_send(l + 1, 0, 1, full).wait_recv()

            @pl.when(low_ok)
            def _():
                chain_send(l + 1, 0, 0, full).wait_recv()

            bq[...] = bq[...] - got_b[l + 1, 0] - got_b[l + 1, 1]
            xb[l + 1, own] = bq[...]
            for p in range(1, m):
                spread(l + 1, p).start()

            @pl.when(low_ok)
            def _():
                chain_send(l + 1, 0, 1, full).wait_send()
                chain_send(l + 1, 2, 1, full).wait_send()

            @pl.when(up_ok)
            def _():
                chain_send(l + 1, 0, 0, full).wait_send()
                chain_send(l + 1, 2, 0, full).wait_send()

            @pl.when(jnp.logical_and(low_ok, l + 1 < levels))
            def _():
                chain_send(l + 1, 1, 1, full).wait_send()

            @pl.when(jnp.logical_and(up_ok, l + 1 < levels))
            def _():
                chain_send(l + 1, 1, 0, full).wait_send()

            for p in range(1, m):
                spread_fg(l, p).wait_send()

        return full

    lax.fori_loop(0, levels + 1, level, 1)

    sol[...] = dot_nn(hq[2], work[...])

    def sol_copy():
        return copy(sol, got_sol, s_sol.at[0], s_sol.at[1], lax.rem(k + 1, n), x)

    @pl.when(has_up)
    def _():
        sol_copy().start()

    @pl.when(jnp.logical_not(has_low))
    def _():
        zero(got_sol)

    out[2] = sol[...]
    part1 = hq[1] - dot_nn(sol[...], g1[...])

    @pl.when(has_low)
    def _():
        sol_copy().wait_recv()

    x1 = dot_nn(part1 - dot_nn(got_sol[...], f1[...]), inv1[...])
    out[1] = x1
    part0 = loads[0] - dot_nn(got_sol[...], gath[4])
    out[0] = dot_nn(part0 - dot_nn(x1, c0t[...]), inv0[...])

    @pl.when(has_up)
    def _():
        sol_copy().wait_send()
        c2_copy().wait_send()

    for i in range(5):
        for p in range(1, m):
            first(i, sources[i], p).wait_send()


def per_device(n, m, diagonal_blocks, couplings, right_sides):
    levels = n.bit_length() - 1
    slabs, q, size = diagonal_blocks.shape
    nrhs = right_sides.shape[0]
    loads = jnp.swapaxes(right_sides, 0, 1)
    steps = levels + 1

    def vmem(*shape):
        return pltpu.VMEM(shape, jnp.float32)

    def dma(*shape):
        return pltpu.SemaphoreType.DMA(shape)

    space = pl.BlockSpec(memory_space=pltpu.VMEM)
    result = pl.pallas_call(
        functools.partial(kernel, n, m, levels),
        out_shape=jax.ShapeDtypeStruct(loads.shape, jnp.float32),
        in_specs=[space] * 3,
        out_specs=space,
        scratch_shapes=[
            vmem(5, size, size), vmem(size, size), vmem(size, size), vmem(size, size),
            vmem(size, size), vmem(size, size), vmem(size, size), vmem(size, size), vmem(size, size),
            vmem(slabs, nrhs, size), vmem(q, size), vmem(q, size), vmem(nrhs, size),
            vmem(2, q, size), vmem(2, q, size), vmem(2, nrhs, size),
            vmem(steps, 2, q, size), vmem(steps, 2, nrhs, size),
            vmem(steps, size, size), vmem(steps, 2, size, size),
            vmem(nrhs, size), vmem(nrhs, size),
            dma(5, m - 1), dma(5, m - 1), dma(2), dma(2),
            dma(3, 2), dma(2, m - 1),
            dma(steps, 2), dma(steps, 2), dma(steps, 2), dma(steps, m - 1), dma(steps, m - 1),
        ],
        compiler_params=pltpu.CompilerParams(
            collective_id=0, has_side_effects=True, vmem_limit_bytes=40 * 1024 * 1024
        ),
    )(diagonal_blocks, couplings, loads)
    return jnp.swapaxes(result, 0, 1)


def solution(mesh):
    n, m = mesh.shape["chain"], mesh.shape["col"]
    return jax.shard_map(
        functools.partial(per_device, n, m),
        mesh=mesh,
        in_specs=(P("chain", "col", None), P("chain", "col", None), P("col", "chain", None)),
        out_specs=P("col", "chain", None),
        check_vma=False,
    )
```

time: 934 us -> 192 us (0.21); the launches traced: 921 us -> 192 us
  other arithmetic: 490 us -> 0 us
  Pallas kernels: 0 us -> 189 us
  starting transfers between devices: 155 us -> 0 us
  blocking collectives: 148 us -> 0 us
  local copies, waits for them, and re-layouts: 56.2 us -> 3.27 us
  matrix products: 47.9 us -> 0 us
  between operations: 13.9 us -> 0.01 us
    another operation x87 -> x0, other arithmetic: 489 us -> none  [the longest x55 276 us: invert(): lower_factor = jnp.linalg.cholesky(matrix)]
    pallas_call x0 -> x1, Pallas kernels: none -> 189 us  [per_device(): pl.pallas_call(functools.partial(kernel, n, m, levels), out_shape=jax.Sha...]
    ppermute x33 -> x0, starting transfers between devices: 155 us -> none  [passed_along(): return lax.ppermute(shard, axis, pairs)]
    all_gather x15 -> x0, blocking collectives: 148 us -> none  [the longest x6 57.8 us: per_device(): lax.all_gather(b_part, 'col', axis=1, tiled=True)]
    another operation x86 -> x0, local copies, waits for them, and re-layouts: 39.6 us -> none  [the longest x58 35.5 us: invert(): return jax.scipy.linalg.cho_solve((lower_factor, True), identity)]
    dot_general x71 -> x0, matrix products: 28.7 us -> none  [matmul(): return jnp.dot(first_factor, second_factor, precision=finest)]
    another operation x72 -> x0, matrix products: 19.2 us -> none  [the longest x48 13.7 us: invert(): return jax.scipy.linalg.cho_solve((lower_factor, True), identity)]
    unnamed x65 -> x7, local copies, waits for them, and re-layouts: 13.4 us -> 3.27 us
  transfers between devices with their start and end apart: 33 -> 0, of which waited for: 4 -> 0; matrix products, arithmetic and copies ran while one was open for 22% -> 0% of each run, Pallas kernels for 0% -> 0%
where the time goes in v1:
time: 192 us
  Pallas kernels  189 us (98%)
  local copies, waits for them, and re-layouts  3.27 us (2%)
    pallas_call x1, Pallas kernels, per_device(): pl.pallas_call(functools.partial(kernel, n, m, levels), out_shape=jax.Sha...  189 us

profile of v1, /device:TPU:1, one launch (start us, length us, event | category | flops | bytes accessed | tf_op | source)
XLA Modules:
  0.0 192.2 jit_solution(174391207424600028)
XLA Ops:
  0.0 0.0 copy-start
  0.0 0.9 copy-done
  0.9 0.0 copy-start.1
  0.9 0.9 copy-done.1
  1.9 0.0 copy-start.2
  1.9 0.8 copy-done.2
  2.7 188.9 %shard_map.37 = f32[3,16,256]{2,1,0:T(8,128)S(1)} custom-call(f32[3,64,256]{2,1,0:T(8,128)S(1)} %copy-done, f32[3,64,256]{2,1,0:T(8,128)S(1)} %copy-done.1, f32[3,16,256]{2,1,0:T(8,128)S(1)} %bitcast.3), custom_call_target="tpu_custom_call" | custom-call | tf_op jit(solution)/shard_map/pallas_call | solution.py:454
  191.6 0.6 copy.5
Async XLA Ops:
  0.0 0.9 copy-start
  0.9 0.9 copy-start.1
  1.9 0.8 copy-start.2
